TPU v7x, 32 devices: a whole 2x2x4 slice. The times are simulated.
32 devices in a mesh: dom: 8 (over z, y), grp: 4 (over x, core).
Axes of the slice: x: 2, y: 2, z: 4, core: 2. Of those that a mesh axis runs over, the one named last changes fastest.
Arguments:
- nodes: bfloat16 [4, 4096, 128], P('grp', 'dom'), may hold values from -6 to 6
- edges: bfloat16 [4, 32, 128, 128], P('grp', 'dom'), may hold values from -6 to 6
- senders: int32 [4, 32, 128], P('grp', 'dom'), may hold values from 0 to 767
- receivers: int32 [4, 32, 128], P('grp', 'dom'), may hold values from 0 to 511
- block_count: int32 [4, 8], P('grp', 'dom'), may hold values from 1 to 4
- send_rows: int32 [4, 8, 2, 128], P('grp', 'dom'), may hold values from 0 to 511
- node_cot: bfloat16 [4, 4096, 128], P('grp', 'dom'), may hold values from -6 to 6
- edge_cot: bfloat16 [4, 32, 128, 128], P('grp', 'dom'), may hold values from -6 to 6
- edge_w1: bfloat16 [384, 128], replicated, may hold values from -0.3125 to 0.3125
- edge_b1: float32 [128], replicated, may hold values from -3 to 3
- edge_w2: bfloat16 [128, 128], replicated, may hold values from -0.5 to 0.5
- edge_b2: float32 [128], replicated, may hold values from -3 to 3
- edge_gain: float32 [128], replicated, may hold values from 0.5 to 1.5
- edge_shift: float32 [128], replicated, may hold values from -3 to 3
- node_w1: bfloat16 [256, 128], replicated, may hold values from -0.375 to 0.375
- node_b1: float32 [128], replicated, may hold values from -3 to 3
- node_w2: bfloat16 [128, 128], replicated, may hold values from -0.5 to 0.5
- node_b2: float32 [128], replicated, may hold values from -3 to 3
- node_gain: float32 [128], replicated, may hold values from 0.5 to 1.5
- node_shift: float32 [128], replicated, may hold values from -3 to 3
Outputs:
- node_out: bfloat16 [4, 4096, 128], P('grp', 'dom')
- edge_out: bfloat16 [4, 32, 128, 128], P('grp', 'dom')
- grad_node: bfloat16 [4, 4096, 128], P('grp', 'dom')
- grad_edge: bfloat16 [4, 32, 128, 128], P('grp', 'dom')
- weight_grads: float32 [115712], replicated
Inputs may be any that keep to these rules, and one draw needn't show every extreme that they name: `senders`: rows below 512 are the device's own nodes; row 512 + k holds the k-th row sent by the lower neighbouring partition, row 640 + k the k-th row sent by the upper one. `receivers`: receivers are own nodes of the device that holds the edge. `block_count`: A device's live blocks are its first ones; the rest are padding. send_rows[g, d, 0, :] are own rows of device d sent to device d - 1 of group g, send_rows[g, d, 1, :] those sent to device d + 1; they may repeat; lists toward no device are unused.
All inputs are finite; a program needn't handle non-finite values.
Results may differ from a plain program's by a relative error of at most 0.0054.
Values may be sent and summed in bfloat16 or wider, within the bound.
A program may use at most 64 MiB of HBM per device.

v0:
```python
import math
import jax
import jax.numpy as jnp
from jax import lax
from jax.sharding import PartitionSpec as P

EPSILON = 1e-05


def extended(value, sides, width):
    for axis, dim in sides:
        size, length = (lax.axis_size(axis), value.shape[dim])
        up = [(i, (i + 1) % size) for i in range(size - 1)]
        down = [(j, i) for i, j in up]
        last = lax.slice_in_dim(value, length - width, length, axis=dim)
        leading = lax.slice_in_dim(value, 0, width, axis=dim)
        before = lax.ppermute(last, axis, up)
        after = lax.ppermute(leading, axis, down)
        value = jnp.concatenate([before, value, after], axis=dim)
    return value


def norm_forward(pre_norm, norm_gain, norm_shift):
    average = jnp.mean(pre_norm, axis=-1, keepdims=True)
    centred = pre_norm - average
    variance = jnp.mean(centred * centred, axis=-1, keepdims=True)
    inverse = lax.rsqrt(variance + EPSILON)
    normed = centred * inverse
    return (normed * norm_gain + norm_shift, normed, inverse)


def norm_backward(grad_out, normed, inverse, norm_gain):
    scaled = grad_out * norm_gain
    return inverse * (
        scaled
        - jnp.mean(scaled, axis=-1, keepdims=True)
        - normed * jnp.mean(scaled * normed, axis=-1, keepdims=True)
    )


def silu_slope(pre_act):
    sigmoid = jax.nn.sigmoid(pre_act)
    return sigmoid * (1.0 + pre_act * (1.0 - sigmoid))


def row_product(left, right):
    return lax.dot_general(
        left, right, (((0,), (0,)), ((), ())), preferred_element_type=jnp.float32
    )


def mlp_forward(inputs, weights):
    w_first, b_first, w_second, b_second, norm_gain, norm_shift = weights
    first_pre = jnp.dot(inputs, w_first, preferred_element_type=jnp.float32) + b_first
    hidden = jax.nn.silu(first_pre).astype(jnp.bfloat16)
    second_pre = jnp.dot(hidden, w_second, preferred_element_type=jnp.float32) + b_second
    output, normed, inverse = norm_forward(second_pre, norm_gain, norm_shift)
    return (output, (first_pre, hidden, normed, inverse))


def mlp_backward(inputs, saved, grad_out, weights):
    w_first, b_first, w_second, b_second, norm_gain, norm_shift = weights
    first_pre, hidden, normed, inverse = saved
    grad_second = norm_backward(grad_out, normed, inverse, norm_gain)
    second_low = grad_second.astype(jnp.bfloat16)
    grad_hidden = jnp.dot(second_low, w_second.T, preferred_element_type=jnp.float32)
    grad_first = grad_hidden * silu_slope(first_pre)
    first_low = grad_first.astype(jnp.bfloat16)
    grad_inputs = jnp.dot(first_low, w_first.T, preferred_element_type=jnp.float32)
    grads = (
        row_product(inputs, first_low),
        jnp.sum(grad_first, axis=0),
        row_product(hidden, second_low),
        jnp.sum(grad_second, axis=0),
        jnp.sum(grad_out * normed, axis=0),
        jnp.sum(grad_out, axis=0),
    )
    return (grad_inputs, grads)


def shards(
    nodes,
    edges,
    senders,
    receivers,
    block_count,
    send_rows,
    node_cot,
    edge_cot,
    edge_w1,
    edge_b1,
    edge_w2,
    edge_b2,
    edge_gain,
    edge_shift,
    node_w1,
    node_b1,
    node_w2,
    node_b2,
    node_gain,
    node_shift,
):
    edge_weights = (edge_w1, edge_b1, edge_w2, edge_b2, edge_gain, edge_shift)
    node_weights = (node_w1, node_b1, node_w2, node_b2, node_gain, node_shift)
    own_nodes = nodes[0]
    node_rows, width = own_nodes.shape
    block_total = senders.shape[1]
    block_rows = senders.shape[2]
    edge_rows = block_total * block_rows
    flat_edges = edges[0].reshape(edge_rows, width)
    flat_send = senders[0].reshape(edge_rows)
    flat_recv = receivers[0].reshape(edge_rows)
    flat_cot = edge_cot[0].reshape(edge_rows, width)
    live_blocks = block_count[0, 0]
    row_lists = send_rows[0, 0]
    slot_count = row_lists.shape[1]
    outgoing = own_nodes[row_lists.reshape(-1)].reshape(2, slot_count, width)
    padded = extended(outgoing, (("dom", 0),), 1)
    from_lower, from_upper = (padded[0], padded[3])
    node_table = jnp.concatenate([own_nodes, from_lower, from_upper], axis=0)
    group_blocks = 4
    span = group_blocks * block_rows
    step_total = (live_blocks + group_blocks - 1) // group_blocks

    def edge_indices(offset):
        positions = offset + jnp.arange(span, dtype=jnp.int32)
        live_mask = (positions // block_rows < live_blocks).astype(jnp.float32)[:, None]
        return (flat_send, flat_recv, live_mask)

    def edge_inputs(send_part, recv_part):
        return jnp.concatenate([flat_edges, node_table[send_part], own_nodes[recv_part]], axis=1)

    stores = ()

    def forward_step(step_index, state_tuple):
        aggregate, edge_out, kept = state_tuple
        offset = step_index * span
        send_part, recv_part, live_mask = edge_indices(offset)
        inputs = edge_inputs(send_part, recv_part)
        message, saved = mlp_forward(inputs, edge_weights)
        live_message = message * live_mask
        aggregate = aggregate.at[recv_part].add(live_message)
        updated = (inputs[:, :width].astype(jnp.float32) + live_message).astype(jnp.bfloat16)
        edge_out = updated
        kept = tuple(
            (
                lax.dynamic_update_slice_in_dim(buffer, piece, offset, 0)
                for buffer, piece in zip(kept, (inputs,) + saved)
            )
        )
        return (aggregate, edge_out, kept)

    aggregate, edge_out, kept = lax.fori_loop(
        0,
        step_total,
        forward_step,
        (jnp.zeros((node_rows, width), jnp.float32), flat_edges, stores),
    )
    node_inputs = jnp.concatenate([own_nodes, aggregate.astype(jnp.bfloat16)], axis=1)
    update, node_saved = mlp_forward(node_inputs, node_weights)
    node_out = (own_nodes.astype(jnp.float32) + update).astype(jnp.bfloat16)
    node_grad = node_cot[0].astype(jnp.float32)
    grad_node_inputs, node_grads = mlp_backward(node_inputs, node_saved, node_grad, node_weights)
    grad_aggregate = grad_node_inputs[:, width:]

    def backward_step(step_index, state_tuple):
        table_grad, grad_edge, totals = state_tuple
        offset = step_index * span
        send_part, recv_part, live_mask = edge_indices(offset)
        inputs = edge_inputs(send_part, recv_part)
        unused_output, saved = mlp_forward(inputs, edge_weights)
        cot_part = flat_cot.astype(jnp.float32)
        grad_message = live_mask * (cot_part + grad_aggregate[recv_part])
        grad_inputs, step_grads = mlp_backward(inputs, saved, grad_message, edge_weights)
        new_grad = (cot_part + grad_inputs[:, :width]).astype(jnp.bfloat16)
        grad_edge = new_grad
        table_grad = table_grad.at[send_part].add(grad_inputs[:, width : 2 * width])
        table_grad = table_grad.at[recv_part].add(grad_inputs[:, 2 * width :])
        totals = tuple((total + piece for total, piece in zip(totals, step_grads)))
        return (table_grad, grad_edge, totals)

    zero_grads = tuple((jnp.zeros(piece.shape, jnp.float32) for piece in edge_weights))
    table_grad, grad_edge, edge_grads = lax.fori_loop(
        0,
        step_total,
        backward_step,
        (jnp.zeros((node_table.shape[0], width), jnp.float32), flat_cot, zero_grads),
    )
    halo_grad = table_grad[node_rows:].reshape(2, slot_count, width)
    padded_grad = extended(halo_grad.astype(jnp.bfloat16), (("dom", 0),), 1).astype(halo_grad.dtype)
    back_lower, back_upper = (padded_grad[0], padded_grad[3])
    returned = jnp.concatenate([back_lower, back_upper], axis=0)
    local_grad = node_grad + grad_node_inputs[:, :width] + table_grad[:node_rows]
    local_grad = local_grad.at[row_lists.reshape(-1)].add(returned)
    grad_node = local_grad.astype(jnp.bfloat16)
    flat_grads = jnp.concatenate([piece.reshape(-1) for piece in edge_grads + node_grads])
    summed = lax.psum(flat_grads, ("dom", "grp"))
    scale = 1.0 / math.sqrt(lax.axis_size("dom") * lax.axis_size("grp") * edge_rows)
    weight_grads = summed * scale
    return (
        node_out[None],
        edge_out.reshape(1, block_total, block_rows, width),
        grad_node[None],
        grad_edge.reshape(1, block_total, block_rows, width),
        weight_grads,
    )


def solution(mesh):
    return jax.shard_map(
        shards,
        mesh=mesh,
        in_specs=(
            P("grp", "dom", None),
            P("grp", "dom", None, None),
            P("grp", "dom", None),
            P("grp", "dom", None),
            P("grp", "dom"),
            P("grp", "dom", None, None),
            P("grp", "dom", None),
            P("grp", "dom", None, None),
            P(),
            P(),
            P(),
            P(),
            P(),
            P(),
            P(),
            P(),
            P(),
            P(),
            P(),
            P(),
        ),
        out_specs=(
            P("grp", "dom", None),
            P("grp", "dom", None, None),
            P("grp", "dom", None),
            P("grp", "dom", None, None),
            P(),
        ),
        check_vma=False,
    )
```

profile of v0, /device:TPU:0, one launch (start us, length us, event | category | flops | bytes accessed | tf_op | source)
XLA Modules:
  0.0 210.2 jit_solution(15320110725477557572)
XLA Ops:
  7.9 1.6 gather_fusion.1
  9.7 1.3 collective-permute-start.1
  11.1 5.7 %collective-permute-start = (bf16[1,128,128]{1,2,0:T(8,128)(2,1)S(1)}, bf16[1,128,128]{1,2,0:T(8,128)(2,1)S(1)}, u32[]{:S(2)}, u32[]{:S(2)}) collective-permute-start(bf16[1,128,128]{1,2,0:T(8,128)(2,1)S(1)} %bitcast.159), channel_id=1, source_target_pairs={{0,4},{4,8},{8,12},{12,16},{16,20},{20,24},{24,28},{1,5},{5,9},{9,... | collective-permute-start | bytes 98312 | tf_op jit(solution)/shard_map/ppermute | solution.py:17
  17.6 0.7 convert_reduce_fusion
  19.2 1.3 gather_fusion.3
  22.5 1.3 gather_fusion.2
  25.3 5.3 %while.42 = (s32[]{:T(128)}, f32[512,128]{1,0:T(8,128)S(1)}, bf16[512,128]{1,0:T(8,128)(2,1)}, s32[]{:T(128)}, s32[512]{0:T(512)S(1)}, /*index=5*/f32[128]{0:T(1...) while((s32[]{:T(128)}, f32[512,128]{1,0:T(8,128)S(1)}, ...), condition=%wide.region_4.5_spmd, body=%wide.region_2.4_spmd.sunk | while | flops 1060867 | bytes 1078433 | solution.py:153
  26.0 0.9 add_convert_fusion.3
  26.9 3.7 %scatter_custom_fusion.15 = f32[512,128]{1,0:T(8,128)S(1)} fusion(f32[512,128]{1,0:T(8,128)S(1)} %get-tuple-element.1141, s32[512]{0:T(512)S(1)} %bitcast.155, f32[512,128]{1,0:T(8,128)S(1)} %get-tuple-element.1161, f32[512]{0:T(512)S(1)} %fusion.116, f32[128]{0:T(128)S(1)} %get-tuple-element.1165, f32[128]{0:T(128)S(1)} %get-tuple-element.1164, ...), kind=kCustom, calls=%fused_computation.11.clone.1 | custom fusion | flops 458752 | bytes 531968 | tf_op jit(solution)/shard_map/while/body/scatter-add | solution.py:142
  33.1 0.9 convolution_bitcast_fusion.1
  34.1 0.8 fusion.78
  34.9 0.9 convolution_bitcast_fusion
  36.0 0.7 fusion.73
  36.7 1.0 gather_fusion.4
  40.1 17.7 %while.43 = (s32[]{:T(128)}, f32[768,128]{1,0:T(8,128)S(1)}, bf16[512,128]{0,1:T(8,128)(2,1)}, f32[384,128]{1,0:T(8,128)S(1)}, f32[128]{0:T(128)}, /*index=5*/f3...) while((s32[]{:T(128)}, f32[768,128]{1,0:T(8,128)S(1)}, ...), condition=%wide.region_20.21_spmd, body=%wide.region_9.20_spmd.sunk | while | flops 204813824 | bytes 10293525 | solution.py:183
  41.0 1.3 gather_fusion
  43.4 1.1 add.621
  44.5 1.3 add.622
  45.8 1.1 add.623
  47.2 1.0 fusion.132
  48.5 1.1 add.620
  50.8 3.5 %scatter_custom_fusion.18 = f32[768,128]{1,0:T(8,128)S(1)} fusion(f32[768,128]{1,0:T(8,128)S(1)} %get-tuple-element.1196, s32[512]{0:T(512)S(1)} %bitcast.147, f32[512,384]{1,0:T(8,128)S(1)} %fusion.133), kind=kCustom, calls=%fused_computation.43.clone.1 | custom fusion | flops 65536 | bytes 655360 | tf_op jit(solution)/shard_map/while/body/scatter-add | solution.py:177
  54.3 3.5 %scatter_custom_fusion.19 = f32[768,128]{1,0:T(8,128)S(1)} fusion(f32[768,128]{1,0:T(8,128)S(1)} %scatter_custom_fusion.18, s32[512]{0:T(512)S(1)} %bitcast.154, f32[512,384]{1,0:T(8,128)S(1)} %fusion.133), kind=kCustom, calls=%fused_computation.41.clone.1 | custom fusion | flops 65536 | bytes 655360 | tf_op jit(solution)/shard_map/while/body/scatter-add | solution.py:178
  58.0 0.8 copy-done.4
  59.0 4.8 %collective-permute-start.2 = (bf16[1,128,128]{2,1,0:T(8,128)(2,1)S(1)}, bf16[1,128,128]{2,1,0:T(8,128)(2,1)S(1)}, u32[]{:S(2)}, u32[]{:S(2)}) collective-permute-start(bf16[1,128,128]{2,1,0:T(8,128)(2,1)S(1)} %get-tuple-element.858), channel_id=1, source_target_pairs={{0,4},{4,8},{8,12},{12,16},{16,20},{20,24},{24,28},{1,5},{5,9},{9,... | collective-permute-start | bytes 98312 | tf_op jit(solution)/shard_map/ppermute | solution.py:17
  63.8 1.3 collective-permute-start.3
  70.4 0.8 copy.61
  71.1 0.8 copy.62
  72.1 0.8 slice-done
  72.9 2.1 scatter_custom_fusion.3
  75.6 125.9 %all-reduce.2.cloned.1.call-done = f32[115712]{0:T(1024)} async-done(((f32[115712]{0:T(1024)}), f32[115712]{0:T(1024)}) %all-reduce.2.cloned.1.call-update) | async-done | bytes 462864 | tf_op jit(solution)/shard_map/psum | solution.py:197
  201.5 1.8 broadcast_multiply_fusion.4
  (146 shorter events, 20.6 us)
Async XLA Ops:
  7.2 23.5 %copy-start = (bf16[256,128]{1,0:T(8,128)(2,1)S(1)}, bf16[256,128]{1,0:T(8,128)(2,1)}, u32[]{:S(2)}) copy-start(bf16[256,128]{1,0:T(8,128)(2,1)} %param.38) | copy-start | bytes 196612
  7.2 0.7 copy-start.20
  7.2 194.4 %all-reduce.2.cloned.1.call-start = ((), (), s32[]{:S(2)}) async-start(), calls=%async_computation | async-start | bytes 925696 | tf_op jit(solution)/shard_map/psum | solution.py:197
  9.6 7.9 %copy-start.10 = (bf16[1,512,128]{2,1,0:T(8,128)(2,1)S(1)}, bf16[1,512,128]{2,1,0:T(8,128)(2,1)}, u32[]{:S(2)}) copy-start(bf16[1,512,128]{2,1,0:T(8,128)(2,1)} %param.30) | copy-start | bytes 393220
  9.7 12.6 %collective-permute-start.1 = (bf16[1,128,128]{1,2,0:T(8,128)(2,1)S(1)}, bf16[1,128,128]{1,2,0:T(8,128)(2,1)S(1)}, u32[]{:S(2)}, u32[]{:S(2)}) collective-permute-start(bf16[1,128,128]{1,2,0:T(8,128)(2,1)S(1)} %bitcast.158), channel_id=1, source_target_pairs={{4,0},{8,4},{12,8},{16,12},{20,16},{24,20},{28,24},{5,1},{9,5},{13... | collective-permute-start | bytes 98312 | tf_op jit(solution)/shard_map/ppermute | solution.py:18
  11.1 5.7 %copy-start.8 = (s32[1,4,128]{2,1,0:T(4,128)S(1)}, s32[1,4,128]{2,1,0:T(4,128)}, u32[]{:S(2)}) copy-start(s32[1,4,128]{2,1,0:T(4,128)} %param.27) | copy-start | bytes 6148
  11.1 11.1 %collective-permute-start = (bf16[1,128,128]{1,2,0:T(8,128)(2,1)S(1)}, bf16[1,128,128]{1,2,0:T(8,128)(2,1)S(1)}, u32[]{:S(2)}, u32[]{:S(2)}) collective-permute-start(bf16[1,128,128]{1,2,0:T(8,128)(2,1)S(1)} %bitcast.159), channel_id=1, source_target_pairs={{0,4},{4,8},{8,12},{12,16},{16,20},{20,24},{24,28},{1,5},{5,9},{9,... | collective-permute-start | bytes 98312 | tf_op jit(solution)/shard_map/ppermute | solution.py:17
  16.8 0.7 copy-start.13
  17.6 1.4 copy-start.1
  19.1 1.4 copy-start.11
  20.6 1.0 copy-start.2
  22.4 1.4 copy-start.3
  22.4 1.4 copy-start.15
  22.5 1.4 copy-start.17
  22.5 1.4 copy-start.25
  24.6 0.7 copy-start.9
  24.6 0.7 copy-start.16
  30.6 0.7 copy-start.23
  31.2 0.8 copy-start.24
  31.3 0.8 copy-start.27
  54.3 3.5 %copy-start.26 = (bf16[128,128]{1,0:T(8,128)(2,1)S(1)}, bf16[128,128]{1,0:T(8,128)(2,1)}, u32[]{:S(2)}) copy-start(bf16[128,128]{1,0:T(8,128)(2,1)} %get-tuple-element.1286) | copy-start | bytes 98308 | tf_op jit(solution)/shard_map/while
  57.8 12.1 %copy-start.6 = (bf16[768,128]{1,0:T(8,128)(2,1)}, bf16[768,128]{1,0:T(8,128)(2,1)S(1)}, u32[]{:S(2)}) copy-start(bf16[768,128]{1,0:T(8,128)(2,1)S(1)} %convert.3) | copy-start | bytes 589828
  57.8 1.0 copy-start.4
  59.0 13.1 %collective-permute-start.2 = (bf16[1,128,128]{2,1,0:T(8,128)(2,1)S(1)}, bf16[1,128,128]{2,1,0:T(8,128)(2,1)S(1)}, u32[]{:S(2)}, u32[]{:S(2)}) collective-permute-start(bf16[1,128,128]{2,1,0:T(8,128)(2,1)S(1)} %get-tuple-element.858), channel_id=1, source_target_pairs={{0,4},{4,8},{8,12},{12,16},{16,20},{20,24},{24,28},{1,5},{5,9},{9,... | collective-permute-start | bytes 98312 | tf_op jit(solution)/shard_map/ppermute | solution.py:17
  63.8 8.3 %collective-permute-start.3 = (bf16[1,128,128]{2,1,0:T(8,128)(2,1)S(1)}, bf16[1,128,128]{2,1,0:T(8,128)(2,1)S(1)}, u32[]{:S(2)}, u32[]{:S(2)}) collective-permute-start(bf16[1,128,128]{2,1,0:T(8,128)(2,1)S(1)} %get-tuple-element.859), channel_id=1, source_target_pairs={{4,0},{8,4},{12,8},{16,12},{20,16},{24,20},{28,24},{5,1},{9,5},{13... | collective-permute-start | bytes 98312 | tf_op jit(solution)/shard_map/ppermute | solution.py:18
  65.1 2.6 %copy-start.12 = (f32[32768]{0:T(1024)S(1)}, f32[32768]{0:T(1024)}, u32[]{:S(2)}) copy-start(f32[32768]{0:T(1024)} %convolution_bitcast_fusion) | copy-start | bytes 393220
  67.7 0.8 copy-start.14
  68.6 0.7 copy-start.21
  69.2 0.7 copy-start.22
  69.5 0.9 copy-start.7
  69.9 2.1 %copy-start.5 = (f32[115712]{0:T(1024)}, f32[115712]{0:T(1024)S(1)}, u32[]{:S(2)}) copy-start(f32[115712]{0:T(1024)S(1)} %constant_dynamic-update-slice_fusion.3) | copy-start | bytes 1388548
  72.0 0.8 slice-start
  (3 other events, 1.9 us)
Sparse Core Ops, SparseCore 0:
  72.2 129.3 all-reduce.1
where the time goes:
time: 211 us; the launch traced here: 210 us
  waiting for transfers between devices  126 us (60%)
  local copies, waits for them, and re-layouts  24.7 us (12%)
  other arithmetic  24.5 us (12%)
  between operations  15.3 us (7%)
  starting transfers between devices  13.1 us (6%)
  matrix products  6.24 us (3%)
    psum x1, waiting for transfers between devices, shards(): summed = lax.psum(flat_grads, ('dom', 'grp'))  126 us
    unnamed x75, local copies, waits for them, and re-layouts  12.4 us
    ppermute x2, starting transfers between devices, extended(): before = lax.ppermute(last, axis, up)  10.5 us
    add x4, other arithmetic, backward_step(): totals = tuple((total + piece for total, piece in zip(totals, step_grads)))  4.61 us
  transfers between devices with their start and end apart: 5, of which 1 were waited for; matrix products, arithmetic and copies ran while one was open for 5% of the time, Pallas kernels for 0%

commit v1 on v0

--- a/solution.py
+++ b/solution.py
@@ -194,7 +194,7 @@
     local_grad = local_grad.at[row_lists.reshape(-1)].add(returned)
     grad_node = local_grad.astype(jnp.bfloat16)
     flat_grads = jnp.concatenate([piece.reshape(-1) for piece in edge_grads + node_grads])
-    summed = lax.psum(flat_grads, ("dom", "grp"))
+    summed = lax.psum(lax.psum(flat_grads, "grp"), "dom")
     scale = 1.0 / math.sqrt(lax.axis_size("dom") * lax.axis_size("grp") * edge_rows)
     weight_grads = summed * scale
     return (

time: 211 us -> 184 us (0.87)
  waiting for transfers between devices: 126 us -> 101 us
    psum x1 -> x2, waiting for transfers between devices: 126 us -> 98.6 us  [shards(): summed = lax.psum(lax.psum(flat_grads, 'grp'), 'dom')]
    ppermute x2, waiting for transfers between devices: 0.01 us -> 2.83 us  [extended(): after = lax.ppermute(leading, axis, down)]
  transfers between devices with their start and end apart: 5 -> 6, of which waited for: 1 -> 3; matrix products, arithmetic and copies ran while one was open for 5% -> 4% of each run, Pallas kernels for 0% -> 0%
where the time goes in v1:
time: 184 us; the launch traced here: 183 us
  waiting for transfers between devices  101 us (55%)
  other arithmetic  24.5 us (13%)
  local copies, waits for them, and re-layouts  23.5 us (13%)
  between operations  15.3 us (8%)
  starting transfers between devices  11.8 us (6%)
  matrix products  6.24 us (3%)
    psum x2, waiting for transfers between devices, shards(): summed = lax.psum(lax.psum(flat_grads, 'grp'), 'dom')  98.6 us
    unnamed x75, local copies, waits for them, and re-layouts  12.7 us
    ppermute x2, starting transfers between devices, extended(): before = lax.ppermute(last, axis, up)  9.18 us
    add x4, other arithmetic, backward_step(): totals = tuple((total + piece for total, piece in zip(totals, step_grads)))  4.61 us
  transfers between devices with their start and end apart: 6, of which 3 were waited for; matrix products, arithmetic and copies ran while one was open for 4% of the time, Pallas kernels for 0%

profile of v1, /device:TPU:0, one launch (start us, length us, event | category | flops | bytes accessed | tf_op | source)
XLA Modules:
  0.0 183.3 jit_solution(12328088851232060005)
XLA Ops:
  7.9 1.6 gather_fusion.1
  9.7 1.3 collective-permute-start.1
  11.1 5.7 %collective-permute-start = (bf16[1,128,128]{1,2,0:T(8,128)(2,1)S(1)}, bf16[1,128,128]{1,2,0:T(8,128)(2,1)S(1)}, u32[]{:S(2)}, u32[]{:S(2)}) collective-permute-start(bf16[1,128,128]{1,2,0:T(8,128)(2,1)S(1)} %bitcast.159), channel_id=1, source_target_pairs={{0,4},{4,8},{8,12},{12,16},{16,20},{20,24},{24,28},{1,5},{5,9},{9,... | collective-permute-start | bytes 98312 | tf_op jit(solution)/shard_map/ppermute | solution.py:17
  19.2 1.3 gather_fusion.3
  22.5 1.3 gather_fusion.2
  25.3 5.3 %while.42 = (s32[]{:T(128)}, f32[512,128]{1,0:T(8,128)S(1)}, bf16[512,128]{1,0:T(8,128)(2,1)}, s32[]{:T(128)}, s32[512]{0:T(512)S(1)}, /*index=5*/f32[128]{0:T(1...) while((s32[]{:T(128)}, f32[512,128]{1,0:T(8,128)S(1)}, ...), condition=%wide.region_4.5_spmd, body=%wide.region_2.4_spmd.sunk | while | flops 1060867 | bytes 1078433 | solution.py:153
  26.0 0.9 add_convert_fusion.3
  26.9 3.7 %scatter_custom_fusion.15 = f32[512,128]{1,0:T(8,128)S(1)} fusion(f32[512,128]{1,0:T(8,128)S(1)} %get-tuple-element.1141, s32[512]{0:T(512)S(1)} %bitcast.155, f32[512,128]{1,0:T(8,128)S(1)} %get-tuple-element.1161, f32[512]{0:T(512)S(1)} %fusion.116, f32[128]{0:T(128)S(1)} %get-tuple-element.1165, f32[128]{0:T(128)S(1)} %get-tuple-element.1164, ...), kind=kCustom, calls=%fused_computation.11.clone.1 | custom fusion | flops 458752 | bytes 531968 | tf_op jit(solution)/shard_map/while/body/scatter-add | solution.py:142
  33.1 0.9 convolution_bitcast_fusion.1
  34.1 0.8 fusion.78
  34.9 0.9 convolution_bitcast_fusion
  36.0 1.0 gather_fusion.4
  37.2 0.8 copy.69
  40.2 17.7 %while.43 = (s32[]{:T(128)}, f32[768,128]{1,0:T(8,128)S(1)}, bf16[512,128]{0,1:T(8,128)(2,1)}, f32[384,128]{1,0:T(8,128)S(1)}, f32[128]{0:T(128)}, /*index=5*/f3...) while((s32[]{:T(128)}, f32[768,128]{1,0:T(8,128)S(1)}, ...), condition=%wide.region_20.21_spmd, body=%wide.region_9.20_spmd.sunk | while | flops 204813824 | bytes 10293525 | solution.py:183
  41.1 1.3 gather_fusion
  43.6 1.1 add.623
  44.7 1.3 add.624
  46.0 1.1 add.625
  47.3 1.0 fusion.132
  48.7 1.1 add.622
  50.9 3.5 %scatter_custom_fusion.18 = f32[768,128]{1,0:T(8,128)S(1)} fusion(f32[768,128]{1,0:T(8,128)S(1)} %get-tuple-element.1196, s32[512]{0:T(512)S(1)} %bitcast.147, f32[512,384]{1,0:T(8,128)S(1)} %fusion.133), kind=kCustom, calls=%fused_computation.43.clone.1 | custom fusion | flops 65536 | bytes 655360 | tf_op jit(solution)/shard_map/while/body/scatter-add | solution.py:177
  54.4 3.5 %scatter_custom_fusion.19 = f32[768,128]{1,0:T(8,128)S(1)} fusion(f32[768,128]{1,0:T(8,128)S(1)} %scatter_custom_fusion.18, s32[512]{0:T(512)S(1)} %bitcast.154, f32[512,384]{1,0:T(8,128)S(1)} %fusion.133), kind=kCustom, calls=%fused_computation.41.clone.1 | custom fusion | flops 65536 | bytes 655360 | tf_op jit(solution)/shard_map/while/body/scatter-add | solution.py:178
  63.0 0.8 copy-done.5
  63.9 34.6 %all-reduce.3.cloned.1.call-done = f32[115712]{0:T(1024)} async-done(((f32[115712]{0:T(1024)}), f32[115712]{0:T(1024)}) %all-reduce.3.cloned.1.call-update) | async-done | bytes 462864 | tf_op jit(solution)/shard_map/psum | solution.py:197
  98.5 3.5 %collective-permute-start.2 = (bf16[1,128,128]{2,1,0:T(8,128)(2,1)S(1)}, bf16[1,128,128]{2,1,0:T(8,128)(2,1)S(1)}, u32[]{:S(2)}, u32[]{:S(2)}) collective-permute-start(bf16[1,128,128]{2,1,0:T(8,128)(2,1)S(1)} %get-tuple-element.858), channel_id=1, source_target_pairs={{0,4},{4,8},{8,12},{12,16},{16,20},{20,24},{24,28},{1,5},{5,9},{9,... | collective-permute-start | bytes 98312 | tf_op jit(solution)/shard_map/ppermute | solution.py:17
  102.0 1.3 collective-permute-start.3
  103.3 0.8 copy.61
  104.1 0.8 copy.62
  105.0 2.8 %collective-permute-done.3 = bf16[1,128,128]{2,1,0:T(8,128)(2,1)S(1)} collective-permute-done((bf16[1,128,128]{2,1,0:T(8,128)(2,1)S(1)}, bf16[1,128,128]{2,1,0:T(8,128)(2,1)S(1)}, u32[]{:S(2)}, u32[]{:S(2)}) %collective-permute-start.3) | collective-permute-done | bytes 32800 | tf_op jit(solution)/shard_map/ppermute | solution.py:18
  107.9 2.1 %scatter_custom_fusion.3 = f32[512,128]{1,0:T(8,128)S(1)} fusion(f32[512,128]{1,0:T(8,128)S(1)} %copy.60, s32[256]{0:T(256)S(1)} %bitcast.163, f32[128,128]{1,0:T(8,128)S(1)} %get-tuple-element.862, f32[]{:T(128)} %constant.240, f32[128,128]{1,0:T(8,128)S(1)} %get-tuple-element.861), kind=kCustom, calls=%fused_computation.117 | custom fusion | flops 65536 | bytes 393220 | tf_op jit(solution)/shard_map/scatter-add | solution.py:194
  110.6 64.0 %all-reduce.5.cloned.1.call-done = f32[115712]{0:T(1024)} async-done(((f32[115712]{0:T(1024)}), f32[115712]{0:T(1024)}) %all-reduce.5.cloned.1.call-update) | async-done | bytes 462864 | tf_op jit(solution)/shard_map/psum | solution.py:197
  174.6 1.8 broadcast_multiply_fusion.4
  (149 shorter events, 20.9 us)
Async XLA Ops:
  7.2 23.5 %copy-start = (bf16[256,128]{1,0:T(8,128)(2,1)S(1)}, bf16[256,128]{1,0:T(8,128)(2,1)}, u32[]{:S(2)}) copy-start(bf16[256,128]{1,0:T(8,128)(2,1)} %param.38) | copy-start | bytes 196612
  7.2 0.7 copy-start.20
  7.2 91.3 %all-reduce.3.cloned.1.call-start = ((), (), s32[]{:S(2)}) async-start(), calls=%async_computation | async-start | bytes 925696 | tf_op jit(solution)/shard_map/psum | solution.py:197
  9.6 7.9 %copy-start.10 = (bf16[1,512,128]{2,1,0:T(8,128)(2,1)S(1)}, bf16[1,512,128]{2,1,0:T(8,128)(2,1)}, u32[]{:S(2)}) copy-start(bf16[1,512,128]{2,1,0:T(8,128)(2,1)} %param.30) | copy-start | bytes 393220
  9.7 12.6 %collective-permute-start.1 = (bf16[1,128,128]{1,2,0:T(8,128)(2,1)S(1)}, bf16[1,128,128]{1,2,0:T(8,128)(2,1)S(1)}, u32[]{:S(2)}, u32[]{:S(2)}) collective-permute-start(bf16[1,128,128]{1,2,0:T(8,128)(2,1)S(1)} %bitcast.158), channel_id=1, source_target_pairs={{4,0},{8,4},{12,8},{16,12},{20,16},{24,20},{28,24},{5,1},{9,5},{13... | collective-permute-start | bytes 98312 | tf_op jit(solution)/shard_map/ppermute | solution.py:18
  11.1 5.7 %copy-start.8 = (s32[1,4,128]{2,1,0:T(4,128)S(1)}, s32[1,4,128]{2,1,0:T(4,128)}, u32[]{:S(2)}) copy-start(s32[1,4,128]{2,1,0:T(4,128)} %param.27) | copy-start | bytes 6148
  11.1 11.1 %collective-permute-start = (bf16[1,128,128]{1,2,0:T(8,128)(2,1)S(1)}, bf16[1,128,128]{1,2,0:T(8,128)(2,1)S(1)}, u32[]{:S(2)}, u32[]{:S(2)}) collective-permute-start(bf16[1,128,128]{1,2,0:T(8,128)(2,1)S(1)} %bitcast.159), channel_id=1, source_target_pairs={{0,4},{4,8},{8,12},{12,16},{16,20},{20,24},{24,28},{1,5},{5,9},{9,... | collective-permute-start | bytes 98312 | tf_op jit(solution)/shard_map/ppermute | solution.py:17
  16.8 0.7 copy-start.13
  17.6 1.4 copy-start.1
  19.1 1.4 copy-start.11
  20.6 1.0 copy-start.2
  22.4 1.4 copy-start.3
  22.4 1.4 copy-start.15
  22.5 1.4 copy-start.17
  22.5 1.4 copy-start.25
  24.6 0.7 copy-start.9
  24.6 0.7 copy-start.16
  31.2 0.8 copy-start.24
  31.3 0.8 copy-start.27
  54.4 3.5 %copy-start.26 = (bf16[128,128]{1,0:T(8,128)(2,1)S(1)}, bf16[128,128]{1,0:T(8,128)(2,1)}, u32[]{:S(2)}) copy-start(bf16[128,128]{1,0:T(8,128)(2,1)} %get-tuple-element.1290) | copy-start | bytes 98308 | tf_op jit(solution)/shard_map/while
  58.1 3.3 %copy-start.14 = (f32[16384]{0:T(1024)S(1)}, f32[16384]{0:T(1024)}, u32[]{:S(2)}) copy-start(f32[16384]{0:T(1024)} %convolution_bitcast_fusion.1) | copy-start | bytes 196612
  58.1 2.6 %copy-start.12 = (f32[32768]{0:T(1024)S(1)}, f32[32768]{0:T(1024)}, u32[]{:S(2)}) copy-start(f32[32768]{0:T(1024)} %convolution_bitcast_fusion) | copy-start | bytes 393220
  58.8 2.7 %copy-start.4 = (f32[512,128]{0,1:T(8,128)S(1)}, f32[512,128]{0,1:T(8,128)}, u32[]{:S(2)}) copy-start(f32[512,128]{0,1:T(8,128)} %copy.69) | copy-start | bytes 786436
  61.4 0.7 copy-start.21
  62.3 0.7 copy-start.22
  63.0 0.8 copy-start.5
  63.8 110.8 %all-reduce.5.cloned.1.call-start = ((), (), s32[]{:S(2)}) async-start(), calls=%async_computation.1 | async-start | bytes 925696 | tf_op jit(solution)/shard_map/psum | solution.py:197
  63.9 39.5 %copy-start.6 = (bf16[768,128]{1,0:T(8,128)(2,1)}, bf16[768,128]{1,0:T(8,128)(2,1)S(1)}, u32[]{:S(2)}) copy-start(bf16[768,128]{1,0:T(8,128)(2,1)S(1)} %convert.3) | copy-start | bytes 589828
  98.5 4.9 %copy-start.7 = (bf16[512,128]{0,1:T(8,128)(2,1)S(1)}, bf16[512,128]{0,1:T(8,128)(2,1)}, u32[]{:S(2)}) copy-start(bf16[512,128]{0,1:T(8,128)(2,1)} %get-tuple-element.1267) | copy-start | bytes 393220
  98.5 6.5 %collective-permute-start.2 = (bf16[1,128,128]{2,1,0:T(8,128)(2,1)S(1)}, bf16[1,128,128]{2,1,0:T(8,128)(2,1)S(1)}, u32[]{:S(2)}, u32[]{:S(2)}) collective-permute-start(bf16[1,128,128]{2,1,0:T(8,128)(2,1)S(1)} %get-tuple-element.858), channel_id=1, source_target_pairs={{0,4},{4,8},{8,12},{12,16},{16,20},{20,24},{24,28},{1,5},{5,9},{9,... | collective-permute-start | bytes 98312 | tf_op jit(solution)/shard_map/ppermute | solution.py:17
  102.0 5.8 %collective-permute-start.3 = (bf16[1,128,128]{2,1,0:T(8,128)(2,1)S(1)}, bf16[1,128,128]{2,1,0:T(8,128)(2,1)S(1)}, u32[]{:S(2)}, u32[]{:S(2)}) collective-permute-start(bf16[1,128,128]{2,1,0:T(8,128)(2,1)S(1)} %get-tuple-element.859), channel_id=1, source_target_pairs={{4,0},{8,4},{12,8},{16,12},{20,16},{24,20},{28,24},{5,1},{9,5},{13... | collective-permute-start | bytes 98312 | tf_op jit(solution)/shard_map/ppermute | solution.py:18
  104.9 3.0 %slice-start = ((bf16[768,128]{1,0:T(8,128)(2,1)}), bf16[256,128]{1,0:T(8,128)(2,1)S(1)}, s32[]{:S(2)}) async-start(bf16[768,128]{1,0:T(8,128)(2,1)} %copy-done.6), calls=%async_computation.2 | async-start | bytes 131072 | tf_op jit(solution)/shard_map/slice | solution.py:189
  (4 other events, 2.6 us)
Sparse Core Ops, SparseCore 0:
  63.9 34.4 all-reduce.2
  101.9 72.7 all-reduce.4
